TPU v7x, 32 devices: a whole 2x2x4 slice. The times are simulated.
32 devices in a mesh: section: 2 (over core), fsdp: 8 (over z, y), tensor: 2 (over x).
Axes of the slice: x: 2, y: 2, z: 4, core: 2. Of those that a mesh axis runs over, the one named last changes fastest.
Arguments:
- inputs: bfloat16 [2, 1024, 1024], P(None, 'fsdp'), may hold values from -6 to 6
- cotangent: float32 [2, 2, 1024, 1024], P('section', None, 'fsdp'), may hold values from -8 to 8
- norm_gains: bfloat16 [2, 2, 1024], P('section', None, 'fsdp'), may hold values from 0.5 to 1.5
- norm_biases: bfloat16 [2, 2, 1024], P('section', None, 'fsdp'), may hold values from -1.796875 to 1.796875
- w_qkv: bfloat16 [2, 1024, 3, 1024], P('section', 'fsdp', None, 'tensor'), may hold values from -0.1875 to 0.1875
- w_out: bfloat16 [2, 1024, 1024], P('section', 'tensor', 'fsdp'), may hold values from -0.75 to 0.75
- w_up: bfloat16 [2, 1024, 4096], P('section', 'fsdp', 'tensor'), may hold values from -0.1875 to 0.1875
- w_down: bfloat16 [2, 4096, 1024], P('section', 'tensor', 'fsdp'), may hold values from -0.09375 to 0.09375
Outputs:
- section_out: bfloat16 [2, 2, 1024, 1024], P('section', None, 'fsdp')
- input_grads: float32 [2, 2, 1024, 1024], P('section', None, 'fsdp')
- gain_grads: float32 [2, 2, 1024], P('section', None, 'fsdp')
- bias_grads: float32 [2, 2, 1024], P('section', None, 'fsdp')
- qkv_grads: float32 [2, 1024, 3, 1024], P('section', 'fsdp', None, 'tensor')
- out_grads: float32 [2, 1024, 1024], P('section', 'tensor', 'fsdp')
- up_grads: float32 [2, 1024, 4096], P('section', 'fsdp', 'tensor')
- down_grads: float32 [2, 4096, 1024], P('section', 'tensor', 'fsdp')
All inputs are finite; a program needn't handle non-finite values.
Results may differ from a plain program's by a relative error of at most 0.014.
Values may be sent and summed in bfloat16 or wider, within the bound.
A program may use at most 128 MiB of HBM per device.

v0:
```python
import math
import jax
import jax.numpy as jnp
from jax import lax
from jax.sharding import PartitionSpec as P

HD = 64
SEQ = 128
EPS = 1e-05


def shifted(x, axis, by):
    peers = lax.axis_size(axis)
    pairs = [(i, i + by) for i in range(peers) if 0 <= i + by < peers]
    return lax.ppermute(x, axis, pairs)


def angles(positions, head_dim):
    rot = head_dim // 4
    half = rot // 2
    freq = 10000.0 ** (-(jnp.arange(half).astype(jnp.float32) * 2.0 / rot))
    theta = positions.astype(jnp.float32)[:, None] * freq[None, :]
    return (jnp.cos(theta), jnp.sin(theta))


def rotate(value, cosine, sine):
    half = cosine.shape[1]
    first = value[..., :half]
    second = value[..., half : 2 * half]
    rest = value[..., 2 * half :]
    cpart = cosine[:, None, :]
    spart = sine[:, None, :]
    return jnp.concatenate(
        [first * cpart - second * spart, second * cpart + first * spart, rest], axis=-1
    )


def normalize(u):
    whole = u.astype(jnp.float32)
    centred = whole - jnp.mean(whole, axis=-1, keepdims=True)
    rstd = lax.rsqrt(jnp.mean(centred * centred, axis=-1, keepdims=True) + EPS)
    return (centred * rstd, rstd)


def gelu_slope(hidden):
    return 0.5 * (1.0 + lax.erf(hidden / math.sqrt(2.0))) + hidden * jnp.exp(
        -0.5 * hidden * hidden
    ) / math.sqrt(2.0 * math.pi)


def grouped(value):
    return value.reshape((value.shape[0] // SEQ, SEQ) + value.shape[1:])


def masked_scores(query, key):
    scores = jnp.einsum("sqhd,skhd->shqk", query, key, preferred_element_type=jnp.float32)
    places = jnp.arange(SEQ, dtype=jnp.int32)
    return jnp.where(places[None, :] <= places[:, None], scores, -1e30)


def attention_forward(query, key, value):
    tokens, heads = (query.shape[0], query.shape[1])
    scores = masked_scores(grouped(query), grouped(key))
    top = jnp.max(scores, axis=-1, keepdims=True)
    lse = top + jnp.log(jnp.sum(jnp.exp(scores - top), axis=-1, keepdims=True))
    probs = jnp.exp(scores - lse).astype(jnp.bfloat16)
    attended = jnp.einsum(
        "shqk,skhd->sqhd", probs, grouped(value), preferred_element_type=jnp.float32
    )
    return (attended.reshape(tokens, heads, HD), lse[..., 0])


def attention_backward(query, key, value, lse, d_att, attended):
    tokens, heads = (query.shape[0], query.shape[1])
    delta = jnp.sum(d_att.astype(jnp.float32) * attended.astype(jnp.float32), axis=-1)
    delta = jnp.swapaxes(grouped(delta), 1, 2)
    query_s, key_s, value_s, grads_s = (
        grouped(query),
        grouped(key),
        grouped(value),
        grouped(d_att),
    )
    probs = jnp.exp(masked_scores(query_s, key_s) - lse[..., None])
    d_probs = jnp.einsum("sqhd,skhd->shqk", grads_s, value_s, preferred_element_type=jnp.float32)
    d_scores = (probs * (d_probs - delta[..., None])).astype(jnp.bfloat16)
    d_query = jnp.einsum("shqk,skhd->sqhd", d_scores, key_s, preferred_element_type=jnp.float32)
    d_key = jnp.einsum("shqk,sqhd->skhd", d_scores, query_s, preferred_element_type=jnp.float32)
    d_value = jnp.einsum(
        "shqk,sqhd->skhd", probs.astype(jnp.bfloat16), grads_s, preferred_element_type=jnp.float32
    )
    shape = (tokens, heads, HD)
    return (d_query.reshape(shape), d_key.reshape(shape), d_value.reshape(shape))


def layer_forward(u, params):
    gains, biases, wqkv, wout, wup, wdown = params
    tokens, width = u.shape
    local = wqkv.shape[2]
    heads = local // HD
    normed, rstd = normalize(u)
    gain = gains.astype(jnp.float32)
    bias = biases.astype(jnp.float32)
    first = (normed * gain[0] + bias[0]).astype(jnp.bfloat16)
    second = (normed * gain[1] + bias[1]).astype(jnp.bfloat16)
    qkv = jnp.dot(
        first, wqkv.reshape(width, 3 * local), preferred_element_type=jnp.float32
    ).reshape(tokens, 3, heads, HD)
    qpos = jnp.arange(tokens, dtype=jnp.int32) % SEQ
    cosine, sine = angles(qpos, HD)
    query = (rotate(qkv[:, 0], cosine, sine) * HD ** (-0.5)).astype(jnp.bfloat16)
    key = rotate(qkv[:, 1], cosine, sine).astype(jnp.bfloat16)
    value = qkv[:, 2].astype(jnp.bfloat16)
    attended, lse = attention_forward(query, key, value)
    attended = attended.astype(jnp.bfloat16).reshape(tokens, local)
    hidden = jnp.dot(second, wup, preferred_element_type=jnp.float32)
    act = jax.nn.gelu(hidden, approximate=False).astype(jnp.bfloat16)
    branch = jnp.dot(attended, wout, preferred_element_type=jnp.float32) + jnp.dot(
        act, wdown, preferred_element_type=jnp.float32
    )
    total = lax.psum(branch, "tensor")
    result = (u.astype(jnp.float32) + total).astype(jnp.bfloat16)
    return (result, (normed, rstd, first, second, query, key, value, attended, lse, hidden, act))


def layer_backward(grad, saved, params):
    normed, rstd, first, second, query, key, value, attended, lse, hidden, act = saved
    gains, biases, wqkv, wout, wup, wdown = params
    tokens, width = grad.shape
    local = wqkv.shape[2]
    heads = local // HD
    grad_half = grad.astype(jnp.bfloat16)
    d_down = jnp.dot(act.T, grad_half, preferred_element_type=jnp.float32)
    d_act = jnp.dot(grad_half, wdown.T, preferred_element_type=jnp.float32)
    d_hidden = (d_act * gelu_slope(hidden)).astype(jnp.bfloat16)
    d_up = jnp.dot(second.T, d_hidden, preferred_element_type=jnp.float32)
    d_second = jnp.dot(d_hidden, wup.T, preferred_element_type=jnp.float32)
    d_wout = jnp.dot(attended.T, grad_half, preferred_element_type=jnp.float32)
    d_att = (
        jnp.dot(grad_half, wout.T, preferred_element_type=jnp.float32)
        .astype(jnp.bfloat16)
        .reshape(tokens, heads, HD)
    )
    d_query, d_key, d_value = attention_backward(
        query, key, value, lse, d_att, attended.reshape(tokens, heads, HD)
    )
    qpos = jnp.arange(tokens, dtype=jnp.int32) % SEQ
    cosine, sine = angles(qpos, HD)
    dq_back = rotate(d_query * HD ** (-0.5), cosine, -sine)
    dk_back = rotate(d_key, cosine, -sine)
    d_qkv = (
        jnp.stack([dq_back, dk_back, d_value], axis=1)
        .astype(jnp.bfloat16)
        .reshape(tokens, 3 * local)
    )
    d_wqkv = jnp.dot(first.T, d_qkv, preferred_element_type=jnp.float32).reshape(width, 3, local)
    d_first = jnp.dot(d_qkv, wqkv.reshape(width, 3 * local).T, preferred_element_type=jnp.float32)
    d_first, d_second = lax.psum((d_first, d_second), "tensor")
    gain = gains.astype(jnp.float32)
    d_gains = jnp.stack([jnp.sum(d_first * normed, axis=0), jnp.sum(d_second * normed, axis=0)])
    d_biases = jnp.stack([jnp.sum(d_first, axis=0), jnp.sum(d_second, axis=0)])
    d_norm = d_first * gain[0] + d_second * gain[1]
    d_input = grad + rstd * (
        d_norm
        - jnp.mean(d_norm, axis=-1, keepdims=True)
        - normed * jnp.mean(d_norm * normed, axis=-1, keepdims=True)
    )
    return (d_input, (d_gains, d_biases, d_wqkv, d_wout, d_up, d_down))


def shards(inputs, cotangent, norm_gains, norm_biases, w_qkv, w_out, w_up, w_down):
    section = lax.axis_index("section")
    micro = inputs.shape[0]
    gathered = (
        lax.all_gather(norm_gains, "fsdp", axis=2, tiled=True),
        lax.all_gather(norm_biases, "fsdp", axis=2, tiled=True),
        lax.all_gather(w_qkv, "fsdp", axis=1, tiled=True),
        lax.all_gather(w_out, "fsdp", axis=2, tiled=True),
        lax.all_gather(w_up, "fsdp", axis=1, tiled=True),
        lax.all_gather(w_down, "fsdp", axis=2, tiled=True),
    )
    params = tuple((piece[0] for piece in gathered))
    received = jnp.zeros(inputs.shape[1:], jnp.bfloat16)
    store = None
    for tick in range(micro + 1):
        index = tick - section
        slot = jnp.clip(index, 0, micro - 1)
        valid = (index >= 0) & (index < micro)
        own = inputs[min(tick, micro - 1)]
        entering = jnp.where(section == 0, own, received)
        result, saved = layer_forward(entering, params)
        record = (result,) + saved
        if store is None:
            store = tuple((jnp.stack([item] * micro) for item in record))
        else:
            store = tuple(
                (
                    jnp.where(valid, lax.dynamic_update_index_in_dim(buffer, item, slot, 0), buffer)
                    for buffer, item in zip(store, record)
                )
            )
        if tick < micro:
            received = shifted(result, "section", 1)
    regathered = (
        lax.all_gather(norm_gains, "fsdp", axis=2, tiled=True),
        lax.all_gather(norm_biases, "fsdp", axis=2, tiled=True),
        lax.all_gather(w_qkv, "fsdp", axis=1, tiled=True),
        lax.all_gather(w_out, "fsdp", axis=2, tiled=True),
        lax.all_gather(w_up, "fsdp", axis=1, tiled=True),
        lax.all_gather(w_down, "fsdp", axis=2, tiled=True),
    )
    again = tuple((piece[0] for piece in regathered))
    incoming = jnp.zeros(inputs.shape[1:], jnp.float32)
    totals = None
    grads_in = None
    for tick in range(micro + 1):
        index = tick - 1 + section
        slot = jnp.clip(index, 0, micro - 1)
        valid = (index >= 0) & (index < micro)
        record = tuple(
            (lax.dynamic_index_in_dim(buffer, slot, 0, keepdims=False) for buffer in store)
        )
        grad = lax.dynamic_index_in_dim(cotangent[0], slot, 0, keepdims=False) + jnp.where(
            section == 0, incoming, 0.0
        )
        d_input, pieces = layer_backward(grad, record[1:], again)
        pieces = tuple((jnp.where(valid, piece, 0.0) for piece in pieces))
        if totals is None:
            totals = pieces
            grads_in = jnp.stack([d_input] * micro)
        else:
            totals = tuple((left + right for left, right in zip(totals, pieces)))
        grads_in = jnp.where(
            valid, lax.dynamic_update_index_in_dim(grads_in, d_input, slot, 0), grads_in
        )
        if tick < micro:
            incoming = shifted(d_input, "section", -1)
    gain_total, bias_total, qkv_total, out_total, up_total, down_total = totals
    summed = (
        lax.psum_scatter(gain_total[None], "fsdp", scatter_dimension=2, tiled=True),
        lax.psum_scatter(bias_total[None], "fsdp", scatter_dimension=2, tiled=True),
        lax.psum_scatter(qkv_total[None], "fsdp", scatter_dimension=1, tiled=True),
        lax.psum_scatter(out_total[None], "fsdp", scatter_dimension=2, tiled=True),
        lax.psum_scatter(up_total[None], "fsdp", scatter_dimension=1, tiled=True),
        lax.psum_scatter(down_total[None], "fsdp", scatter_dimension=2, tiled=True),
    )
    return (
        store[0][None],
        grads_in[None],
        summed[0],
        summed[1],
        summed[2],
        summed[3],
        summed[4],
        summed[5],
    )


def solution(mesh):
    in_specs = (
        P(None, "fsdp", None),
        P("section", None, "fsdp", None),
        P("section", None, "fsdp"),
        P("section", None, "fsdp"),
        P("section", "fsdp", None, "tensor"),
        P("section", "tensor", "fsdp"),
        P("section", "fsdp", "tensor"),
        P("section", "tensor", "fsdp"),
    )
    out_specs = (
        P("section", None, "fsdp", None),
        P("section", None, "fsdp", None),
        P("section", None, "fsdp"),
        P("section", None, "fsdp"),
        P("section", "fsdp", None, "tensor"),
        P("section", "tensor", "fsdp"),
        P("section", "fsdp", "tensor"),
        P("section", "tensor", "fsdp"),
    )
    return jax.shard_map(shards, mesh=mesh, in_specs=in_specs, out_specs=out_specs, check_vma=False)
```

profile of v0, /device:TPU:0, one launch (start us, length us, event | category | flops | bytes accessed | tf_op | source)
XLA Modules:
  0.0 1191.5 jit_solution(10730510585829965908)
XLA Ops:
  7.9 1.9 copy.68
  11.3 22.5 %all_gather.24 = bf16[1,2,1024]{2,1,0:T(2,128)(2,1)S(1)} all-gather(bf16[1,2,128]{2,1,0:T(2,128)(2,1)} %param.11), channel_id=1, replica_groups=mesh['section'=2,'fsdp'=8,'tensor'=2] {'fsdp'}, dimensions={2}, use_global_device_ids=true | all-gather | bytes 4608 | tf_op jit(solution)/shard_map/all_gather | solution.py:175
  33.7 16.7 %all_gather.23 = bf16[1,2,1024]{2,1,0:T(2,128)(2,1)S(1)} all-gather(bf16[1,2,128]{2,1,0:T(2,128)(2,1)} %param.10), channel_id=1, replica_groups=mesh['section'=2,'fsdp'=8,'tensor'=2] {'fsdp'}, dimensions={2}, use_global_device_ids=true | all-gather | bytes 4608 | tf_op jit(solution)/shard_map/all_gather | solution.py:174
  58.1 1.9 convolution_convert_fusion.5
  60.8 55.7 %all-gather.5.cloned.1.call-done = bf16[1,1024,3,512]{1,3,2,0:T(8,128)(2,1)} async-done(((bf16[1,128,3,512]{1,3,2,0:T(8,128)(2,1)}), bf16[1,1024,3,512]{1,3,2,0:T(8,128)(2,1)}) %all-gather.5.cloned.1.call-update) | async-done | bytes 3145744 | tf_op jit(solution)/shard_map/all_gather | solution.py:176
  116.5 2.9 fusion.217
  121.7 67.9 %all-gather.9.cloned.1.call-done = bf16[1,1024,2048]{2,1,0:T(8,128)(2,1)} async-done(((bf16[1,128,2048]{2,1,0:T(8,128)(2,1)}), bf16[1,1024,2048]{2,1,0:T(8,128)(2,1)}) %all-gather.9.cloned.1.call-update) | async-done | bytes 4194320 | tf_op jit(solution)/shard_map/all_gather | solution.py:178
  189.6 5.9 fusion.59
  195.5 69.2 %all-gather.11.cloned.1.call-done = bf16[1,2048,1024]{2,1,0:T(8,128)(2,1)} async-done(((bf16[1,2048,128]{2,1,0:T(8,128)(2,1)}), bf16[1,2048,1024]{2,1,0:T(8,128)(2,1)}) %all-gather.11.cloned.1.call-update) | async-done | bytes 4194320 | tf_op jit(solution)/shard_map/all_gather | solution.py:179
  264.7 2.9 fusion.10
  270.9 3.2 pad_maximum_fusion
  274.1 21.7 %all-reduce.9.cloned.1.call-done = f32[128,1024]{1,0:T(8,128)} async-done(((f32[128,1024]{1,0:T(8,128)}), f32[128,1024]{1,0:T(8,128)}) %all-reduce.9.cloned.1.call-update) | async-done | bytes 524304 | tf_op jit(solution)/shard_map/psum | solution.py:120
  297.0 1.8 collective-permute-start
  306.3 4.9 fusion.152
  314.0 1.6 fusion.250
  315.7 2.8 fusion.80
  318.5 24.3 %all-reduce.11.cloned.1.call-done = f32[128,1024]{1,0:T(8,128)} async-done(((f32[128,1024]{1,0:T(8,128)}), f32[128,1024]{1,0:T(8,128)}) %all-reduce.11.cloned.1.call-update) | async-done | bytes 524304 | tf_op jit(solution)/shard_map/psum | solution.py:120
  342.8 2.7 fusion.192
  345.5 1.9 collective-permute-start.1
  347.4 1.7 fusion.270
  349.1 2.0 fusion.244
  357.8 3.9 fusion.162
  366.0 2.6 fusion.39
  369.4 2.3 fusion.16
  371.9 2.2 fusion.142
  374.6 2.1 fusion.135
  376.7 35.3 %all-reduce.17.cloned.1.call-done = (f32[128,1024]{1,0:T(8,128)}, f32[128,1024]{1,0:T(8,128)}) async-done(((f32[128,1024]{1,0:T(8,128)}, f32[128,1024]{1,0:T(8,128)}), (f32[128,1024]{1,0:T(8,128)}, f32[128,1024]{1,0:T(8,128)})) %all-reduce.17.cloned.1.call-update) | async-done | bytes 1048592 | tf_op jit(solution)/shard_map/psum | solution.py:157
  412.0 1.7 fusion.367
  415.2 1.7 collective-permute-start.2
  425.0 1.5 fusion.52
  426.6 1.8 convolution_bitcast_fusion.3
  431.1 1.4 fusion.382
  432.5 1.6 fusion.36
  435.0 2.3 fusion.14
  437.4 2.3 pad_maximum_fusion.2
  439.7 2.2 fusion.155
  441.9 35.7 %all-reduce.15.cloned.1.call-done = (f32[128,1024]{1,0:T(8,128)}, f32[128,1024]{1,0:T(8,128)}) async-done(((f32[128,1024]{1,0:T(8,128)}, f32[128,1024]{1,0:T(8,128)}), (f32[128,1024]{1,0:T(8,128)}, f32[128,1024]{1,0:T(8,128)})) %all-reduce.15.cloned.1.call-update) | async-done | bytes 1048592 | tf_op jit(solution)/shard_map/psum | solution.py:157
  477.5 1.7 fusion.366
  479.3 2.8 fusion.169
  482.1 1.4 collective-permute-start.3
  492.6 1.5 fusion.51
  494.1 1.8 convolution_bitcast_fusion.1
  498.6 1.4 fusion.383
  500.0 1.6 fusion.33
  502.2 2.3 fusion.12
  504.7 1.7 fusion.275
  506.4 1.8 fusion.273
  508.2 48.9 %all-reduce.13.cloned.1.call-done = (f32[128,1024]{1,0:T(8,128)}, f32[128,1024]{1,0:T(8,128)}, f32[128,1024]{1,0:T(8,128)}) async-done(((f32[128,1024]{1,0:T(8,128)}, f32[128,1024]{1,0:T(8,128)}, f32[128,1024]{1,0:T(8,128)}), (f32[128,1024]{1,0:T(8,128)}, f32[128,1024]{1,0:T(8,128)}, f32[128,1024]{1,0:T(8,128)})) %all-reduce.13.cloned.1.call-update) | async-done | bytes 1572880 | tf_op jit(solution)/shard_map/psum | solution.py:120
  557.1 3.4 fusion.167
  563.0 3.6 add_bitcast_fusion.3
  567.9 2.0 fusion.208
  571.0 4.0 add_bitcast_fusion.2
  578.7 5.3 add_bitcast_fusion.1
  587.8 5.3 add_bitcast_fusion
  594.2 2.3 copy.157
  598.5 2.1 bitcast_dynamic-update-slice_fusion
  600.6 23.8 %reduce-scatter.19.cloned.1.call-done = f32[128,2]{1,0:T(8,128)} async-done(((f32[1024,2]{1,0:T(8,128)}), f32[128,2]{1,0:T(8,128)}) %reduce-scatter.19.cloned.1.call-update) | async-done | bytes 1040
  624.4 1.5 copy.121
  625.8 63.5 %reduce-scatter.21.cloned.1.call-done = f32[128,2]{1,0:T(8,128)} async-done(((f32[1024,2]{1,0:T(8,128)}), f32[128,2]{1,0:T(8,128)}) %reduce-scatter.21.cloned.1.call-update) | async-done | bytes 1040
  689.4 1.5 copy.123
  690.9 70.4 %reduce-scatter.13.cloned.1.call-done = f32[1,512,128]{2,1,0:T(8,128)} async-done(((f32[1,512,1024]{2,1,0:T(8,128)}), f32[1,512,128]{2,1,0:T(8,128)}) %reduce-scatter.13.cloned.1.call-update) | async-done | bytes 262160 | tf_op jit(solution)/shard_map/reduce_scatter | solution.py:242
  761.2 121.7 %reduce-scatter.11.cloned.1.call-done = f32[1,128,3,512]{3,1,2,0:T(8,128)} async-done(((f32[1,1024,3,512]{3,1,2,0:T(8,128)}), f32[1,128,3,512]{3,1,2,0:T(8,128)}) %reduce-scatter.11.cloned.1.call-update) | async-done | bytes 786448 | tf_op jit(solution)/shard_map/reduce_scatter | solution.py:241
  882.9 150.8 %reduce-scatter.15.cloned.1.call-done = f32[1,128,2048]{2,1,0:T(8,128)} async-done(((f32[1,1024,2048]{2,1,0:T(8,128)}), f32[1,128,2048]{2,1,0:T(8,128)}) %reduce-scatter.15.cloned.1.call-update) | async-done | bytes 1048592 | tf_op jit(solution)/shard_map/reduce_scatter | solution.py:243
  1033.7 151.1 %reduce-scatter.17.cloned.1.call-done = f32[1,2048,128]{2,1,0:T(8,128)} async-done(((f32[1,2048,1024]{2,1,0:T(8,128)}), f32[1,2048,128]{2,1,0:T(8,128)}) %reduce-scatter.17.cloned.1.call-update) | async-done | bytes 1048592 | tf_op jit(solution)/shard_map/reduce_scatter | solution.py:244
  (420 shorter events, 79.6 us)
Async XLA Ops:
  7.2 51.0 %all-gather.7.cloned.1.call-start = ((), (), s32[]{:S(2)}) async-start(), calls=%async_computation.7 | async-start | bytes 1179648 | tf_op jit(solution)/shard_map/all_gather | solution.py:177
  7.9 108.6 %all-gather.5.cloned.1.call-start = ((), (), s32[]{:S(2)}) async-start(), calls=%async_computation.6 | async-start | bytes 3538944 | tf_op jit(solution)/shard_map/all_gather | solution.py:176
  9.9 179.7 %all-gather.9.cloned.1.call-start = ((), (), s32[]{:S(2)}) async-start(), calls=%async_computation.8 | async-start | bytes 4718592 | tf_op jit(solution)/shard_map/all_gather | solution.py:178
  10.6 254.1 %all-gather.11.cloned.1.call-start = ((), (), s32[]{:S(2)}) async-start(), calls=%async_computation.9 | async-start | bytes 4718592 | tf_op jit(solution)/shard_map/all_gather | solution.py:179
  11.2 284.6 %all-reduce.9.cloned.1.call-start = ((), (), s32[]{:S(2)}) async-start(), calls=%async_computation.10 | async-start | bytes 1048576 | tf_op jit(solution)/shard_map/psum | solution.py:120
  50.5 70.6 %copy-start.84 = (pred[128,128]{0,1:T(8,128)(4,1)}, pred[128,128]{0,1:T(8,128)(4,1)S(1)}, u32[]{:S(2)}) copy-start(pred[128,128]{0,1:T(8,128)(4,1)S(1)} %iota_compare_fusion) | copy-start | bytes 49156
  54.5 64.9 %copy-start.42 = (bf16[1,128,1024]{2,1,0:T(8,128)(2,1)}, bf16[1,128,1024]{2,1,0:T(8,128)(2,1)S(1)}, u32[]{:S(2)}) copy-start(bf16[1,128,1024]{2,1,0:T(8,128)(2,1)S(1)} %get-tuple-element.59) | copy-start | bytes 786436
  54.5 135.1 %copy-start.56 = (bf16[1,128,1024]{2,1,0:T(8,128)(2,1)}, bf16[1,128,1024]{2,1,0:T(8,128)(2,1)S(1)}, u32[]{:S(2)}) copy-start(bf16[1,128,1024]{2,1,0:T(8,128)(2,1)S(1)} %get-tuple-element.60) | copy-start | bytes 786436
  58.1 61.3 %copy-start.103 = (f32[128,8]{0,1:T(8,128)}, f32[128,8]{0,1:T(8,128)S(1)}, u32[]{:S(2)}) copy-start(f32[128,8]{0,1:T(8,128)S(1)} %get-tuple-element.123) | copy-start | bytes 12292
  121.5 147.3 %copy-start.98 = (f32[8,128]{1,0:T(8,128)}, f32[8,128]{1,0:T(8,128)S(1)}, u32[]{:S(2)}) copy-start(f32[8,128]{1,0:T(8,128)S(1)} %log_add_fusion.2) | copy-start | bytes 12292
  195.5 73.9 %copy-start.62 = (bf16[128,2048]{1,0:T(8,128)(2,1)}, bf16[128,2048]{1,0:T(8,128)(2,1)S(1)}, u32[]{:S(2)}) copy-start(bf16[128,2048]{1,0:T(8,128)(2,1)S(1)} %get-tuple-element.127) | copy-start | bytes 1572868
  195.5 72.1 %copy-start.10 = (bf16[1,512,1024]{2,1,0:T(8,128)(2,1)S(1)}, bf16[1,512,1024]{2,1,0:T(8,128)(2,1)}, u32[]{:S(2)}) copy-start(bf16[1,512,1024]{2,1,0:T(8,128)(2,1)} %all-gather.7.cloned.1.call-done) | copy-start | bytes 3145732
  268.8 74.0 %all-reduce.11.cloned.1.call-start = ((), (), s32[]{:S(2)}) async-start(), calls=%async_computation.11 | async-start | bytes 1048576 | tf_op jit(solution)/shard_map/psum | solution.py:120
  269.4 32.9 %copy-start = (bf16[1,1024,3,512]{1,3,2,0:T(8,128)(2,1)S(1)}, bf16[1,1024,3,512]{1,3,2,0:T(8,128)(2,1)}, u32[]{:S(2)}) copy-start(bf16[1,1024,3,512]{1,3,2,0:T(8,128)(2,1)} %all-gather.5.cloned.1.call-done) | copy-start | bytes 9437188
  296.9 5.4 copy-start.54
  297.0 4.0 collective-permute-start
  300.1 4.9 copy-start.85
  302.0 40.8 %copy-start.18 = (bf16[128,1024]{1,0:T(8,128)(2,1)}, bf16[128,1024]{1,0:T(8,128)(2,1)S(1)}, u32[]{:S(2)}) copy-start(bf16[128,1024]{1,0:T(8,128)(2,1)S(1)} %get-tuple-element.51) | copy-start | bytes 786436
  306.3 5.9 copy-start.74
  306.3 4.9 copy-start.5
  314.0 98.0 %all-reduce.17.cloned.1.call-start = ((), (), s32[]{:S(2)}) async-start(), calls=%async_computation.20 | async-start | bytes 2097152 | tf_op jit(solution)/shard_map/psum | solution.py:157
  315.7 33.4 %copy-start.76 = (bf16[1,128,8,64]{1,3,2,0:T(8,128)(2,1)S(1)}, bf16[1,128,8,64]{1,3,2,0:T(8,128)(2,1)}, u32[]{:S(2)}) copy-start(bf16[1,128,8,64]{1,3,2,0:T(8,128)(2,1)} %copy-done.75) | copy-start | bytes 393220
  345.5 8.2 copy-start.105
  345.5 5.6 collective-permute-start.1
  352.2 5.5 copy-start.108
  352.5 5.3 copy-start.112
  357.8 4.9 copy-start.34
  362.9 5.7 copy-start.35
  369.4 5.2 copy-start.109
  369.4 5.2 copy-start.113
  371.8 45.1 %copy-start.87 = (pred[128,128]{0,1:T(8,128)(4,1)S(1)}, pred[128,128]{0,1:T(8,128)(4,1)}, u32[]{:S(2)}) copy-start(pred[128,128]{0,1:T(8,128)(4,1)} %copy-done.84) | copy-start | bytes 49156
  371.8 45.1 %copy-start.107 = (f32[8,128]{1,0:T(8,128)S(1)}, f32[8,128]{1,0:T(8,128)}, u32[]{:S(2)}) copy-start(f32[8,128]{1,0:T(8,128)} %get-tuple-element.103) | copy-start | bytes 12292
  371.8 105.8 %all-reduce.15.cloned.1.call-start = ((), (), s32[]{:S(2)}) async-start(), calls=%async_computation.19 | async-start | bytes 2097152 | tf_op jit(solution)/shard_map/psum | solution.py:157
  412.0 7.7 copy-start.15
  412.0 8.5 copy-start.12
  415.2 3.8 collective-permute-start.2
  425.0 7.5 copy-start.7
  425.0 7.5 copy-start.36
  425.0 7.5 copy-start.44
  437.3 42.0 %copy-start.121 = (f32[128]{0:T(128)S(1)}, f32[128]{0:T(128)}, u32[]{:S(2)}) copy-start(f32[128]{0:T(128)} %get-tuple-element.120) | copy-start | bytes 1540
  437.3 119.8 %all-reduce.13.cloned.1.call-start = ((), (), s32[]{:S(2)}) async-start(), calls=%async_computation.18 | async-start | bytes 3145728 | tf_op jit(solution)/shard_map/psum | solution.py:120
  477.5 6.0 copy-start.8
  477.5 6.0 copy-start.82
  479.3 5.0 copy-start.22
  479.3 5.0 copy-start.30
  479.3 5.0 copy-start.88
  479.3 5.0 copy-start.106
  479.3 6.1 copy-start.13
  479.3 6.1 copy-start.73
  482.1 4.4 collective-permute-start.3
  492.5 7.5 copy-start.9
  492.5 7.5 copy-start.37
  492.6 7.5 copy-start.40
  504.6 52.6 %copy-start.14 = (f32[2,128,1024]{2,1,0:T(8,128)S(1)}, f32[2,128,1024]{2,1,0:T(8,128)}, u32[]{:S(2)}) copy-start(f32[2,128,1024]{2,1,0:T(8,128)} %fusion.135) | copy-start | bytes 3145732
  504.6 119.8 %reduce-scatter.19.cloned.1.call-start = ((), (), s32[]{:S(2)}) async-start(), calls=%async_computation.16 | async-start | bytes 589824
  508.2 54.8 %copy-start.77 = (bf16[1,128,512]{1,2,0:T(8,128)(2,1)S(1)}, bf16[1,128,512]{1,2,0:T(8,128)(2,1)}, u32[]{:S(2)}) copy-start(bf16[1,128,512]{1,2,0:T(8,128)(2,1)} %get-tuple-element.91) | copy-start | bytes 393220
  561.6 127.8 %reduce-scatter.21.cloned.1.call-start = ((), (), s32[]{:S(2)}) async-start(), calls=%async_computation.17 | async-start | bytes 589824
  562.8 198.4 %reduce-scatter.13.cloned.1.call-start = ((), (), s32[]{:S(2)}) async-start(), calls=%async_computation.13 | async-start | bytes 2359296 | tf_op jit(solution)/shard_map/reduce_scatter | solution.py:242
  566.7 316.2 %reduce-scatter.11.cloned.1.call-start = ((), (), s32[]{:S(2)}) async-start(), calls=%async_computation.12 | async-start | bytes 7077888 | tf_op jit(solution)/shard_map/reduce_scatter | solution.py:241
  575.1 458.6 %reduce-scatter.15.cloned.1.call-start = ((), (), s32[]{:S(2)}) async-start(), calls=%async_computation.14 | async-start | bytes 9437184 | tf_op jit(solution)/shard_map/reduce_scatter | solution.py:243
  584.0 600.7 %reduce-scatter.17.cloned.1.call-start = ((), (), s32[]{:S(2)}) async-start(), calls=%async_computation.15 | async-start | bytes 9437184 | tf_op jit(solution)/shard_map/reduce_scatter | solution.py:244
  593.2 5.3 copy-start.59
  593.2 5.3 copy-start.65
  593.2 5.3 copy-start.116
  (80 other events, 195.1 us)
Sparse Core Ops, SparseCore 0:
  10.0 42.1 all-gather.6
  54.8 61.6 all-gather.4
  118.6 70.9 all-gather.8
  191.5 73.1 all-gather.10
  268.9 26.8 all-reduce.8
  314.1 28.6 all-reduce.10
  371.9 40.0 all-reduce.16
  437.4 40.0 all-reduce.14
  504.7 52.3 all-reduce.12
  561.7 62.5 reduce-scatter.18
  627.7 61.6 reduce-scatter.20
  693.3 67.8 reduce-scatter.12
  765.4 117.4 reduce-scatter.10
  886.9 146.7 reduce-scatter.14
  1037.7 146.9 reduce-scatter.16
where the time goes:
time: 1200 us; the launch traced here: 1190 us
  waiting for transfers between devices  943 us (79%)
  matrix products  95.1 us (8%)
  other arithmetic  59.2 us (5%)
  blocking collectives  39.2 us (3%)
  local copies, waits for them, and re-layouts  31.2 us (3%)
  between operations  16.1 us (1%)
    reduce_scatter x1, waiting for transfers between devices, shards(): lax.psum_scatter(down_total[None], 'fsdp', scatter_dimension=2, tiled=True)  151 us
    reduce_scatter x1, waiting for transfers between devices, shards(): lax.psum_scatter(up_total[None], 'fsdp', scatter_dimension=1, tiled=True)  151 us
    reduce_scatter x1, waiting for transfers between devices, shards(): lax.psum_scatter(qkv_total[None], 'fsdp', scatter_dimension=1, tiled=True)  122 us
    psum x3, waiting for transfers between devices, layer_forward(): total = lax.psum(branch, 'tensor')  94.9 us
    unnamed x17, waiting for transfers between devices  89.4 us
    psum x2, waiting for transfers between devices, layer_backward(): d_first, d_second = lax.psum((d_first, d_second), 'tensor')  71 us
    reduce_scatter x1, waiting for transfers between devices, shards(): lax.psum_scatter(out_total[None], 'fsdp', scatter_dimension=2, tiled=True)  70.4 us
    all_gather x1, waiting for transfers between devices, shards(): lax.all_gather(w_down, 'fsdp', axis=2, tiled=True)  69.2 us
  transfers between devices with their start and end apart: 19, of which 15 were waited for; matrix products, arithmetic and copies ran while one was open for 8% of the time, Pallas kernels for 0%

commit v1 on v0

--- a/solution.py
+++ b/solution.py
@@ -7,6 +7,11 @@
 HD = 64
 SEQ = 128
 EPS = 1e-05
+
+
+def tiled_gather(x, axis, dim):
+    copies = jnp.concatenate([x] * lax.axis_size(axis), axis=dim)
+    return lax.all_to_all(copies, axis, dim, dim, tiled=True)
 
 
 def shifted(x, axis, by):
@@ -176,7 +181,7 @@
         lax.all_gather(w_qkv, "fsdp", axis=1, tiled=True),
         lax.all_gather(w_out, "fsdp", axis=2, tiled=True),
         lax.all_gather(w_up, "fsdp", axis=1, tiled=True),
-        lax.all_gather(w_down, "fsdp", axis=2, tiled=True),
+        tiled_gather(w_down, "fsdp", 2),
     )
     params = tuple((piece[0] for piece in gathered))
     received = jnp.zeros(inputs.shape[1:], jnp.bfloat16)

time: 1200 us -> 1290 us (1.075)
  waiting for transfers between devices: 943 us -> 782 us
  blocking collectives: 39.2 us -> 170 us
  local copies, waits for them, and re-layouts: 31.2 us -> 104 us
  other arithmetic: 59.2 us -> 89.2 us
    all_gather x1, blocking collectives: 22.5 us -> 109 us  [shards(): lax.all_gather(norm_biases, 'fsdp', axis=2, tiled=True)]
    all_gather x1, waiting for transfers between devices: 67.9 us -> 0.01 us  [shards(): lax.all_gather(w_up, 'fsdp', axis=1, tiled=True)]
    all_gather x1, waiting for transfers between devices: 55.7 us -> 0.01 us  [shards(): lax.all_gather(w_qkv, 'fsdp', axis=1, tiled=True)]
    all_gather x1, blocking collectives: 16.7 us -> 60.5 us  [shards(): lax.all_gather(norm_gains, 'fsdp', axis=2, tiled=True)]
    unnamed x0 -> x1, other arithmetic: none -> 26.7 us
    unnamed x257 -> x277, local copies, waits for them, and re-layouts: 24.8 us -> 50.7 us
    concatenate x0 -> x2, local copies, waits for them, and re-layouts: none -> 21.5 us  [tiled_gather(): copies = jnp.concatenate([x] * lax.axis_size(axis), axis=dim)]
    all_to_all x0 -> x1, local copies, waits for them, and re-layouts: none -> 20 us  [tiled_gather(): return lax.all_to_all(copies, axis, dim, dim, tiled=True)]
  transfers between devices with their start and end apart: 19 -> 20, of which waited for: 15 -> 13; matrix products, arithmetic and copies ran while one was open for 8% -> 17% of each run, Pallas kernels for 0% -> 0%
where the time goes in v1:
time: 1290 us; the launch traced here: 1280 us
  waiting for transfers between devices  782 us (61%)
  blocking collectives  170 us (13%)
  local copies, waits for them, and re-layouts  104 us (8%)
  matrix products  99.6 us (8%)
  other arithmetic  89.2 us (7%)
  between operations  16 us (1%)
  starting transfers between devices  15.2 us (1%)
    reduce_scatter x1, waiting for transfers between devices, shards(): lax.psum_scatter(down_total[None], 'fsdp', scatter_dimension=2, tiled=True)  151 us
    reduce_scatter x1, waiting for transfers between devices, shards(): lax.psum_scatter(up_total[None], 'fsdp', scatter_dimension=1, tiled=True)  151 us
    reduce_scatter x1, waiting for transfers between devices, shards(): lax.psum_scatter(qkv_total[None], 'fsdp', scatter_dimension=1, tiled=True)  122 us
    all_gather x1, blocking collectives, shards(): lax.all_gather(norm_biases, 'fsdp', axis=2, tiled=True)  109 us
    unnamed x17, waiting for transfers between devices  89.3 us
    psum x3, waiting for transfers between devices, layer_forward(): total = lax.psum(branch, 'tensor')  79.3 us
    reduce_scatter x1, waiting for transfers between devices, shards(): lax.psum_scatter(out_total[None], 'fsdp', scatter_dimension=2, tiled=True)  70.4 us
    psum x2, waiting for transfers between devices, layer_backward(): d_first, d_second = lax.psum((d_first, d_second), 'tensor')  68.9 us
  transfers between devices with their start and end apart: 20, of which 13 were waited for; matrix products, arithmetic and copies ran while one was open for 17% of the time, Pallas kernels for 0%

profile of v1, /device:TPU:0, one launch (start us, length us, event | category | flops | bytes accessed | tf_op | source)
XLA Modules:
  0.0 1276.5 jit_solution(9383293950246879591)
XLA Ops:
  7.2 2.0 copy.135
  10.0 1.9 constant_dynamic-update-slice_fusion.12
  11.9 1.9 constant_dynamic-update-slice_fusion.11
  13.8 1.9 constant_dynamic-update-slice_fusion.10
  20.1 20.7 %copy.137 = bf16[1,2048,1024]{1,0,2:T(2,128)(2,1)} copy(bf16[1,2048,1024]{2,1,0:T(8,128)(2,1)} %constant_dynamic-update-slice_fusion.5) | data formatting | bytes 8388608 | tf_op jit(solution)/shard_map/concatenate | solution.py:13
  41.3 26.7 %reduce.13 = bf16[1024,2048]{1,0:T(8,128)(2,1)} reduce(bf16[1024,1,2048]{2,1,0:T(2,128)(2,1)} %bitcast.651, bf16[]{:T(256)} %broadcast.873), dimensions={1}, to_apply=%bitcast.580.reduce_sub_computation | reduce | bytes 8388610
  68.0 7.9 reshape.1384
  75.9 7.4 all-to-all-start
  84.1 109.3 %all_gather.23 = bf16[1,2,1024]{2,1,0:T(2,128)(2,1)S(1)} all-gather(bf16[1,2,128]{2,1,0:T(2,128)(2,1)S(1)} %copy-done.125), channel_id=1, replica_groups=mesh['section'=2,'fsdp'=8,'tensor'=2] {'fsdp'}, dimensions={2}, use_global_device_ids=true | all-gather | bytes 4608 | tf_op jit(solution)/shard_map/all_gather | solution.py:180
  193.4 60.5 %all_gather.22 = bf16[1,2,1024]{2,1,0:T(2,128)(2,1)S(1)} all-gather(bf16[1,2,128]{2,1,0:T(2,128)(2,1)S(1)} %copy-done.126), channel_id=1, replica_groups=mesh['section'=2,'fsdp'=8,'tensor'=2] {'fsdp'}, dimensions={2}, use_global_device_ids=true | all-gather | bytes 4608 | tf_op jit(solution)/shard_map/all_gather | solution.py:179
  256.5 3.1 fusion.217
  261.3 8.8 reshape.1385
  270.2 20.0 %copy.138 = bf16[1,2048,1024]{2,1,0:T(8,128)(2,1)} copy(bf16[1,2048,1024]{1,0,2:T(2,128)(2,1)} %bitcast.652) | data formatting | bytes 8388608 | tf_op jit(solution)/shard_map/all_to_all | solution.py:14
  290.2 6.0 fusion.59
  298.5 2.6 convolution_add_fusion.2
  301.2 26.0 %all-reduce.9.cloned.1.call-done = f32[128,1024]{1,0:T(8,128)} async-done(((f32[128,1024]{1,0:T(8,128)}), f32[128,1024]{1,0:T(8,128)}) %all-reduce.9.cloned.1.call-update) | async-done | bytes 524304 | tf_op jit(solution)/shard_map/psum | solution.py:125
  328.4 1.8 collective-permute-start
  336.0 4.9 fusion.152
  345.3 2.3 pad_maximum_fusion.5
  347.6 2.5 pad_maximum_fusion.1
  350.1 2.5 convolution_convert_fusion.5
  361.7 3.1 pad_maximum_fusion
  369.2 4.4 all-reduce.11.cloned.1.call-done
  373.5 2.7 fusion.192
  376.2 1.9 collective-permute-start.1
  378.2 1.7 fusion.270
  379.9 2.1 fusion.244
  387.7 1.8 constant_dynamic-slice_fusion.1
  392.9 3.9 fusion.162
  397.9 2.3 fusion.90
  400.2 49.9 %all-gather.11.cloned.1.call-done = bf16[1,2048,1024]{2,1,0:T(8,128)(2,1)} async-done(((bf16[1,2048,128]{2,1,0:T(8,128)(2,1)}), bf16[1,2048,1024]{2,1,0:T(8,128)(2,1)}) %all-gather.11.cloned.1.call-update) | async-done | bytes 4194320 | tf_op jit(solution)/shard_map/all_gather | solution.py:214
  450.1 4.4 fusion.39
  455.4 2.3 fusion.16
  457.8 2.3 fusion.142
  460.6 2.2 fusion.135
  462.9 33.3 %all-reduce.17.cloned.1.call-done = (f32[128,1024]{1,0:T(8,128)}, f32[128,1024]{1,0:T(8,128)}) async-done(((f32[128,1024]{1,0:T(8,128)}, f32[128,1024]{1,0:T(8,128)}), (f32[128,1024]{1,0:T(8,128)}, f32[128,1024]{1,0:T(8,128)})) %all-reduce.17.cloned.1.call-update) | async-done | bytes 1048592 | tf_op jit(solution)/shard_map/psum | solution.py:162
  496.2 1.7 fusion.367
  499.3 1.7 collective-permute-start.2
  516.1 3.0 fusion.36
  519.9 2.3 fusion.14
  522.3 2.4 pad_maximum_fusion.2
  524.7 2.2 fusion.155
  526.8 35.6 %all-reduce.15.cloned.1.call-done = (f32[128,1024]{1,0:T(8,128)}, f32[128,1024]{1,0:T(8,128)}) async-done(((f32[128,1024]{1,0:T(8,128)}, f32[128,1024]{1,0:T(8,128)}), (f32[128,1024]{1,0:T(8,128)}, f32[128,1024]{1,0:T(8,128)})) %all-reduce.15.cloned.1.call-update) | async-done | bytes 1048592 | tf_op jit(solution)/shard_map/psum | solution.py:162
  562.5 1.7 fusion.366
  564.3 2.8 fusion.169
  584.4 3.0 fusion.33
  587.4 2.3 fusion.12
  589.8 1.7 fusion.275
  591.6 1.8 fusion.273
  593.4 48.9 %all-reduce.13.cloned.1.call-done = (f32[128,1024]{1,0:T(8,128)}, f32[128,1024]{1,0:T(8,128)}, f32[128,1024]{1,0:T(8,128)}) async-done(((f32[128,1024]{1,0:T(8,128)}, f32[128,1024]{1,0:T(8,128)}, f32[128,1024]{1,0:T(8,128)}), (f32[128,1024]{1,0:T(8,128)}, f32[128,1024]{1,0:T(8,128)}, f32[128,1024]{1,0:T(8,128)})) %all-reduce.13.cloned.1.call-update) | async-done | bytes 1572880 | tf_op jit(solution)/shard_map/psum | solution.py:125
  642.3 3.3 fusion.167
  648.1 3.6 add_bitcast_fusion.3
  653.0 2.0 fusion.208
  656.1 4.0 add_bitcast_fusion.2
  663.8 5.3 add_bitcast_fusion.1
  672.9 5.3 add_bitcast_fusion
  679.3 2.3 copy.233
  683.6 2.1 bitcast_dynamic-update-slice_fusion
  685.7 23.8 %reduce-scatter.19.cloned.1.call-done = f32[128,2]{1,0:T(8,128)} async-done(((f32[1024,2]{1,0:T(8,128)}), f32[128,2]{1,0:T(8,128)}) %reduce-scatter.19.cloned.1.call-update) | async-done | bytes 1040
  710.9 63.5 %reduce-scatter.21.cloned.1.call-done = f32[128,2]{1,0:T(8,128)} async-done(((f32[1024,2]{1,0:T(8,128)}), f32[128,2]{1,0:T(8,128)}) %reduce-scatter.21.cloned.1.call-update) | async-done | bytes 1040
  775.9 70.4 %reduce-scatter.13.cloned.1.call-done = f32[1,512,128]{2,1,0:T(8,128)} async-done(((f32[1,512,1024]{2,1,0:T(8,128)}), f32[1,512,128]{2,1,0:T(8,128)}) %reduce-scatter.13.cloned.1.call-update) | async-done | bytes 262160 | tf_op jit(solution)/shard_map/reduce_scatter | solution.py:247
  846.3 121.7 %reduce-scatter.11.cloned.1.call-done = f32[1,128,3,512]{3,1,2,0:T(8,128)} async-done(((f32[1,1024,3,512]{3,1,2,0:T(8,128)}), f32[1,128,3,512]{3,1,2,0:T(8,128)}) %reduce-scatter.11.cloned.1.call-update) | async-done | bytes 786448 | tf_op jit(solution)/shard_map/reduce_scatter | solution.py:246
  967.9 150.8 %reduce-scatter.15.cloned.1.call-done = f32[1,128,2048]{2,1,0:T(8,128)} async-done(((f32[1,1024,2048]{2,1,0:T(8,128)}), f32[1,128,2048]{2,1,0:T(8,128)}) %reduce-scatter.15.cloned.1.call-update) | async-done | bytes 1048592 | tf_op jit(solution)/shard_map/reduce_scatter | solution.py:248
  1118.8 151.0 %reduce-scatter.17.cloned.1.call-done = f32[1,2048,128]{2,1,0:T(8,128)} async-done(((f32[1,2048,1024]{2,1,0:T(8,128)}), f32[1,2048,128]{2,1,0:T(8,128)}) %reduce-scatter.17.cloned.1.call-update) | async-done | bytes 1048592 | tf_op jit(solution)/shard_map/reduce_scatter | solution.py:249
  (446 shorter events, 101.5 us)
Async XLA Ops:
  7.2 8.5 copy-start.4
  7.2 249.3 %all-gather.5.cloned.1.call-start = ((), (), s32[]{:S(2)}) async-start(), calls=%async_computation.7 | async-start | bytes 3538944 | tf_op jit(solution)/shard_map/all_gather | solution.py:181
  9.2 280.9 %all-gather.9.cloned.1.call-start = ((), (), s32[]{:S(2)}) async-start(), calls=%async_computation.9 | async-start | bytes 4718592 | tf_op jit(solution)/shard_map/all_gather | solution.py:183
  75.9 8.2 copy-start.125
  75.9 117.5 %copy-start.126 = (bf16[1,2,128]{2,1,0:T(2,128)(2,1)S(1)}, bf16[1,2,128]{2,1,0:T(2,128)(2,1)}, u32[]{:S(2)}) copy-start(bf16[1,2,128]{2,1,0:T(2,128)(2,1)} %param.10) | copy-start | bytes 1540
  75.9 178.0 %copy-start.32 = (bf16[2,128,1024]{2,1,0:T(8,128)(2,1)S(1)}, bf16[2,128,1024]{2,1,0:T(8,128)(2,1)}, u32[]{:S(2)}) copy-start(bf16[2,128,1024]{2,1,0:T(8,128)(2,1)} %param.8) | copy-start | bytes 1572868
  75.9 185.4 %all-to-all-start = ((bf16[8,2,131072]{2,1,0:T(2,128)(2,1)}), bf16[8,2,131072]{2,1,0:T(2,128)(2,1)}, u32[]{:S(2)}, u32[]{:S(2)}) async-start(bf16[8,2,131072]{2,1,0:T(2,128)(2,1)} %reshape.1384), calls=%async_computation | async-start | bytes 8388608 | tf_op jit(solution)/shard_map/all_to_all | solution.py:14
  83.3 215.2 %all-gather.7.cloned.1.call-start = ((), (), s32[]{:S(2)}) async-start(), calls=%async_computation.8 | async-start | bytes 1179648 | tf_op jit(solution)/shard_map/all_gather | solution.py:182
  84.0 243.2 %all-reduce.9.cloned.1.call-start = ((), (), s32[]{:S(2)}) async-start(), calls=%async_computation.10 | async-start | bytes 1048576 | tf_op jit(solution)/shard_map/psum | solution.py:125
  253.9 7.0 copy-start.84
  254.8 5.9 copy-start.94
  256.5 33.6 %copy-start.53 = (bf16[1,128,1024]{2,1,0:T(8,128)(2,1)}, bf16[1,128,1024]{2,1,0:T(8,128)(2,1)S(1)}, u32[]{:S(2)}) copy-start(bf16[1,128,1024]{2,1,0:T(8,128)(2,1)S(1)} %get-tuple-element.60) | copy-start | bytes 786436
  259.7 10.4 copy-start.88
  259.7 10.4 copy-start.89
  259.7 10.4 copy-start.101
  259.7 10.4 copy-start.102
  261.1 69.1 %copy-start.98 = (f32[8,128]{1,0:T(8,128)}, f32[8,128]{1,0:T(8,128)S(1)}, u32[]{:S(2)}) copy-start(f32[8,128]{1,0:T(8,128)S(1)} %log_add_fusion.2) | copy-start | bytes 12292
  290.1 6.8 copy-start.1
  298.5 34.8 %copy-start = (bf16[1,1024,3,512]{1,3,2,0:T(8,128)(2,1)S(1)}, bf16[1,1024,3,512]{1,3,2,0:T(8,128)(2,1)}, u32[]{:S(2)}) copy-start(bf16[1,1024,3,512]{1,3,2,0:T(8,128)(2,1)} %all-gather.5.cloned.1.call-done) | copy-start | bytes 9437188
  301.2 72.4 %all-reduce.11.cloned.1.call-start = ((), (), s32[]{:S(2)}) async-start(), calls=%async_computation.11 | async-start | bytes 1048576 | tf_op jit(solution)/shard_map/psum | solution.py:125
  328.4 6.2 copy-start.51
  328.4 6.1 copy-start.106
  328.4 3.3 collective-permute-start
  333.1 40.5 %copy-start.17 = (bf16[128,1024]{1,0:T(8,128)(2,1)}, bf16[128,1024]{1,0:T(8,128)(2,1)S(1)}, u32[]{:S(2)}) copy-start(bf16[128,1024]{1,0:T(8,128)(2,1)S(1)} %get-tuple-element.51) | copy-start | bytes 786436
  333.1 7.8 copy-start.111
  333.3 7.6 copy-start.115
  334.4 7.9 copy-start.44
  335.3 6.6 copy-start.90
  335.3 6.6 copy-start.91
  335.3 6.6 copy-start.103
  335.3 6.6 copy-start.104
  344.7 105.4 %all-gather.11.cloned.1.call-start = ((), (), s32[]{:S(2)}) async-start(), calls=%async_computation.12 | async-start | bytes 4718592 | tf_op jit(solution)/shard_map/all_gather | solution.py:214
  345.3 150.9 %all-reduce.17.cloned.1.call-start = ((), (), s32[]{:S(2)}) async-start(), calls=%async_computation.21 | async-start | bytes 2097152 | tf_op jit(solution)/shard_map/psum | solution.py:162
  354.3 10.6 copy-start.52
  354.3 13.0 %copy-start.37 = (f32[128,2048]{1,0:T(8,128)S(1)}, f32[128,2048]{1,0:T(8,128)}, u32[]{:S(2)}) copy-start(f32[128,2048]{1,0:T(8,128)} %get-tuple-element.128) | copy-start | bytes 3145732
  354.3 13.0 %copy-start.79 = (f32[128,2048]{1,0:T(8,128)S(1)}, f32[128,2048]{1,0:T(8,128)}, u32[]{:S(2)}) copy-start(f32[128,2048]{1,0:T(8,128)} %get-tuple-element.131) | copy-start | bytes 3145732
  358.7 9.7 copy-start.72
  376.2 8.3 copy-start.107
  376.2 5.7 collective-permute-start.1
  383.1 9.6 copy-start.109
  383.3 9.3 copy-start.113
  457.7 104.8 %all-reduce.15.cloned.1.call-start = ((), (), s32[]{:S(2)}) async-start(), calls=%async_computation.20 | async-start | bytes 2097152 | tf_op jit(solution)/shard_map/psum | solution.py:162
  496.2 7.8 copy-start.14
  496.2 8.6 copy-start.11
  499.3 3.8 collective-permute-start.2
  509.2 6.9 copy-start.40
  509.2 6.9 copy-start.128
  522.2 42.0 %copy-start.122 = (f32[128]{0:T(128)S(1)}, f32[128]{0:T(128)}, u32[]{:S(2)}) copy-start(f32[128]{0:T(128)} %get-tuple-element.120) | copy-start | bytes 1540
  522.2 120.1 %all-reduce.13.cloned.1.call-start = ((), (), s32[]{:S(2)}) async-start(), calls=%async_computation.19 | async-start | bytes 3145728 | tf_op jit(solution)/shard_map/psum | solution.py:125
  562.5 6.0 copy-start.3
  562.5 6.0 copy-start.82
  564.2 6.1 copy-start.12
  564.3 6.1 copy-start.70
  567.0 4.4 collective-permute-start.3
  577.5 6.9 copy-start.35
  577.5 6.9 copy-start.129
  589.7 52.6 %copy-start.13 = (f32[2,128,1024]{2,1,0:T(8,128)S(1)}, f32[2,128,1024]{2,1,0:T(8,128)}, u32[]{:S(2)}) copy-start(f32[2,128,1024]{2,1,0:T(8,128)} %fusion.135) | copy-start | bytes 3145732
  589.8 119.7 %reduce-scatter.19.cloned.1.call-start = ((), (), s32[]{:S(2)}) async-start(), calls=%async_computation.17 | async-start | bytes 589824
  593.4 54.7 %copy-start.74 = (bf16[1,128,512]{1,2,0:T(8,128)(2,1)S(1)}, bf16[1,128,512]{1,2,0:T(8,128)(2,1)}, u32[]{:S(2)}) copy-start(bf16[1,128,512]{1,2,0:T(8,128)(2,1)} %get-tuple-element.91) | copy-start | bytes 393220
  646.7 127.7 %reduce-scatter.21.cloned.1.call-start = ((), (), s32[]{:S(2)}) async-start(), calls=%async_computation.18 | async-start | bytes 589824
  647.9 198.4 %reduce-scatter.13.cloned.1.call-start = ((), (), s32[]{:S(2)}) async-start(), calls=%async_computation.14 | async-start | bytes 2359296 | tf_op jit(solution)/shard_map/reduce_scatter | solution.py:247
  651.8 316.2 %reduce-scatter.11.cloned.1.call-start = ((), (), s32[]{:S(2)}) async-start(), calls=%async_computation.13 | async-start | bytes 7077888 | tf_op jit(solution)/shard_map/reduce_scatter | solution.py:246
  660.2 458.6 %reduce-scatter.15.cloned.1.call-start = ((), (), s32[]{:S(2)}) async-start(), calls=%async_computation.15 | async-start | bytes 9437184 | tf_op jit(solution)/shard_map/reduce_scatter | solution.py:248
  669.1 600.7 %reduce-scatter.17.cloned.1.call-start = ((), (), s32[]{:S(2)}) async-start(), calls=%async_computation.16 | async-start | bytes 9437184 | tf_op jit(solution)/shard_map/reduce_scatter | solution.py:249
  (86 other events, 254.5 us)
Sparse Core Ops, SparseCore 0:
  10.6 65.3 all-gather.4
  78.1 144.8 all-gather.8
  225.1 37.6 all-gather.6
  301.3 25.8 all-reduce.8
  344.8 28.6 all-reduce.10
  375.4 74.6 all-gather.10
  457.8 38.2 all-reduce.16
  522.3 40.0 all-reduce.14
  589.9 52.3 all-reduce.12
  646.8 62.5 reduce-scatter.18
  712.8 61.5 reduce-scatter.20
  778.4 67.8 reduce-scatter.12
  850.5 117.4 reduce-scatter.10
  972.0 146.7 reduce-scatter.14
  1122.8 146.9 reduce-scatter.16
